TPU v7x, 128 devices: a whole 4x4x4 slice. The times are simulated.
128 devices in a mesh: seq: 32 (over x, y, core), head: 4 (over z).
Axes of the slice: x: 4, y: 4, z: 4, core: 2. Of those that a mesh axis runs over, the one named last changes fastest.
Arguments:
- tokens: bfloat16 [32768, 1536], P('seq', 'head'), may hold values from -6 to 6
- norm_gain: float32 [1536], replicated, may hold values from 0.1 to 1.9
- w_qkv: bfloat16 [1536, 4608], P(None, 'head'), may hold values from -0.15625 to 0.15625
- w_out: bfloat16 [1536, 1536], P('head'), may hold values from -0.15625 to 0.15625
- frame_ids: int32 [32, 16], P('seq'), may hold values from 0 to 7, never falling along the last dimension, each value on 1 to 4 neighbouring positions
- slot_gain: float32 [1536], replicated, may hold values from 0.1 to 1.9
- w_key: bfloat16 [1536, 256], replicated, may hold values from -0.15625 to 0.15625
- w_value: bfloat16 [1536, 256], replicated, may hold values from -0.15625 to 0.15625
- w_query: float32 [256, 256], replicated, may hold values from -0.375 to 0.375
- slot_init: float32 [64, 256], replicated, may hold values from -6 to 6
- w_input: float32 [256, 768], replicated, may hold values from -0.375 to 0.375
- w_hidden: float32 [256, 768], replicated, may hold values from -0.375 to 0.375
Outputs:
- mixed: bfloat16 [32768, 1536], P(('seq', 'head'))
- slots: float32 [64, 256], replicated
Inputs may be any that keep to these rules, and one draw needn't show every extreme that they name: `frame_ids`: ids never fall along a row; a frame covers 1 to 4 blocks, and in every row some frame covers exactly 4 blocks.
All inputs are finite; a program needn't handle non-finite values.
Results may differ from a plain program's by a relative error of at most 0.008.
Values may be sent and summed in bfloat16 or wider, within the bound.
A program may use at most 64 MiB of HBM per device.

v0:
```python
import jax
import jax.numpy as jnp
from jax import lax
from jax.sharding import PartitionSpec as P

HD = 64
ITERS = 3
BLK = 64


def layer_norm(values, gain):
    mean = jnp.mean(values, axis=-1, keepdims=True)
    centred = values - mean
    var = jnp.mean(centred * centred, axis=-1, keepdims=True)
    return centred * lax.rsqrt(var + 1e-06) * gain


def normalize_exp(scores):
    powers = jnp.exp(scores)
    return powers / jnp.sum(powers, axis=-1, keepdims=True)


def recurrent_cell(update, state, w_input, w_hidden):
    high = lax.Precision.HIGHEST
    width = state.shape[1]
    from_in = jnp.dot(update, w_input, precision=high)
    from_state = jnp.dot(state, w_hidden, precision=high)
    reset = jax.nn.sigmoid(from_in[:, :width] + from_state[:, :width])
    gate = jax.nn.sigmoid(from_in[:, width : 2 * width] + from_state[:, width : 2 * width])
    candidate = jnp.tanh(from_in[:, 2 * width :] + reset * from_state[:, 2 * width :])
    return (1.0 - gate) * candidate + gate * state


def local(
    tokens,
    norm_gain,
    w_qkv,
    w_out,
    frame_ids,
    slot_gain,
    w_key,
    w_value,
    w_query,
    slot_init,
    w_input,
    w_hidden,
):
    whole = lax.all_gather(tokens, "head", axis=1, tiled=True)
    tok_count = whole.shape[0]
    normed = layer_norm(whole.astype(jnp.float32), norm_gain).astype(jnp.bfloat16)
    qkv = jnp.dot(normed, w_qkv, preferred_element_type=jnp.float32).astype(jnp.bfloat16)
    heads_here = w_qkv.shape[1] // (3 * HD)
    split = jnp.transpose(qkv.reshape(tok_count, heads_here, 3, HD), (1, 0, 2, 3))
    tok_ids = jnp.repeat(frame_ids[0], BLK)
    same = tok_ids[:, None] == tok_ids[None, :]

    def one_head(head_qkv):
        scores = jnp.dot(
            head_qkv[:, 0, :], head_qkv[:, 1, :].T, preferred_element_type=jnp.float32
        ) * HD ** (-0.5)
        scores = jnp.where(same, scores, -jnp.inf)
        probs = normalize_exp(scores).astype(jnp.bfloat16)
        return jnp.dot(probs, head_qkv[:, 2, :], preferred_element_type=jnp.float32).astype(
            jnp.bfloat16
        )

    outputs = lax.map(one_head, split)
    attended = jnp.transpose(outputs, (1, 0, 2)).reshape(tok_count, heads_here * HD)
    own_rows = tok_count // lax.axis_size("head")
    own_start = lax.axis_index("head") * own_rows
    own = lax.dynamic_slice_in_dim(whole, own_start, own_rows, 0)
    projected = lax.psum_scatter(
        jnp.dot(attended, w_out, preferred_element_type=jnp.float32).astype(jnp.bfloat16),
        "head",
        scatter_dimension=0,
        tiled=True,
    ).astype(jnp.float32)
    mixed = (own.astype(jnp.float32) + projected).astype(jnp.bfloat16)
    slot_in = layer_norm(mixed.astype(jnp.float32), slot_gain).astype(jnp.bfloat16)
    keys = jnp.dot(slot_in, w_key, preferred_element_type=jnp.float32).astype(jnp.bfloat16)
    values = jnp.dot(slot_in, w_value, preferred_element_type=jnp.float32).astype(jnp.bfloat16)
    slots = slot_init
    width = slot_init.shape[1]
    ones = jnp.ones((width,), jnp.float32)
    for step in range(ITERS):
        query = jnp.dot(layer_norm(slots, ones), w_query, precision=lax.Precision.HIGHEST).astype(
            jnp.bfloat16
        )
        logits = jnp.dot(keys, query.T, preferred_element_type=jnp.float32) * width ** (-0.5)
        weights = normalize_exp(logits)
        numer = jnp.einsum(
            "ts,td->sd", weights.astype(jnp.bfloat16), values, preferred_element_type=jnp.float32
        )
        denom = jnp.sum(weights, axis=0)
        numer, denom = lax.psum((numer, denom), ("seq", "head"))
        slots = recurrent_cell(numer / denom[:, None], slots, w_input, w_hidden)
    return (mixed, slots)


def solution(mesh):
    placed = (
        P("seq", "head"),
        P(),
        P(None, "head"),
        P("head", None),
        P("seq", None),
        P(),
        P(),
        P(),
        P(),
        P(),
        P(),
        P(),
    )
    return jax.shard_map(
        local,
        mesh=mesh,
        in_specs=placed,
        out_specs=(P(("seq", "head"), None), P()),
        check_vma=False,
    )
```

profile of v0, /device:TPU:1, one launch (start us, length us, event | category | flops | bytes accessed | tf_op | source)
XLA Modules:
  0.0 575.2 jit_solution(1970555273158845083)
XLA Ops:
  7.2 0.7 all-gather.2.cloned.1.call-update
  8.0 1.0 broadcast_in_dim.14
  9.0 43.7 %all-gather.2.cloned.1.call-done = bf16[1024,1536]{1,0:T(8,128)(2,1)} async-done(((bf16[1024,384]{1,0:T(8,128)(2,1)}), bf16[1024,1536]{1,0:T(8,128)(2,1)}) %all-gather.2.cloned.1.call-update) | async-done | bytes 3145744 | tf_op jit(solution)/shard_map/all_gather | solution.py:48
  52.7 2.5 convert_reduce_fusion
  55.3 0.3 copy-done.1
  55.6 1.0 fusion.12
  56.5 5.8 %convolution_convert_fusion.1 = bf16[1024,1152]{1,0:T(8,128)(2,1)} fusion(bf16[1536,1152]{1,0:T(8,128)(2,1)S(1)} %copy-done, bf16[1024,1536]{1,0:T(8,128)(2,1)S(1)} %copy-done.1, f32[1536]{0:T(1024)S(1)} %copy-done.12, f32[1024]{0:T(1024)S(1)} %add_rsqrt_fusion, f32[1024]{0:T(1024)S(1)} %broadcast_multiply_fusion), kind=kOutput, calls=%fused_computation.23 | convolution fusion | flops 3632922624 | bytes 9058304 | tf_op jit(solution)/shard_map/dot_general | solution.py:51
  62.4 4.3 copy.15
  66.7 23.8 %while.11 = (s32[]{:T(128)}, bf16[6,1024,64]{1,2,0:T(8,128)(2,1)}, bf16[6,1024,3,64]{1,3,2,0:T(8,128)(2,1)}, s32[1024]{0:T(1024)S(1)}, s32[]{:T(128)}) while((s32[]{:T(128)}, bf16[6,1024,64]{1,2,0:T(8,128)(2,1)}, bf16[6,1024,3,64]{1,3,2,0:T(8,128)(2,1)}, s32[1024]{0:T(1024)S(1)}, s32[]{:T(128)}) %tuple.47), condition=%wide.region_4.5_spmd.clone, body=%wide.region_2.4_spmd.clone.sunk | while | flops 277937152 | bytes 9724481 | solution.py:67
  66.7 1.0 dynamic-slice_bitcast_fusion.2
  67.7 1.1 fusion.133
  68.8 1.8 fusion.134
  70.6 1.0 dynamic-slice_bitcast_fusion.2
  71.6 1.1 fusion.133
  72.8 1.8 fusion.134
  74.6 1.0 dynamic-slice_bitcast_fusion.2
  75.6 1.1 fusion.133
  76.7 1.8 fusion.134
  78.6 1.0 dynamic-slice_bitcast_fusion.2
  79.6 1.1 fusion.133
  80.7 1.8 fusion.134
  82.5 1.0 dynamic-slice_bitcast_fusion.2
  83.6 1.1 fusion.133
  84.7 1.8 fusion.134
  86.5 1.0 dynamic-slice_bitcast_fusion.2
  87.5 1.1 fusion.133
  88.6 1.8 fusion.134
  90.5 5.0 convolution_convert_fusion
  95.6 0.9 reduce_sum.157
  96.6 1.0 multiply_reduce_fusion.2
  97.6 1.9 convolution_convert_fusion.6
  99.5 2.4 fusion.102
  102.0 32.3 %reduce-scatter.2.cloned.1.call-done = bf16[256,1536]{1,0:T(8,128)(2,1)} async-done(((bf16[1024,1536]{1,0:T(8,128)(2,1)}), bf16[256,1536]{1,0:T(8,128)(2,1)}) %reduce-scatter.2.cloned.1.call-update) | async-done | bytes 786448 | tf_op jit(solution)/shard_map/reduce_scatter | solution.py:72
  134.3 1.8 convert_reduce_fusion.1
  136.1 0.3 fusion.21
  136.5 0.5 convolution_convert_fusion.3
  137.0 0.5 convolution_convert_fusion.2
  137.7 0.4 copy-done.14
  138.3 0.8 fusion.86
  139.1 0.9 fusion.90
  140.1 64.9 %psum.43 = f32[64]{0:T(128)S(1)} all-reduce(f32[64]{0:T(128)S(1)} %fusion.90), channel_id=1, replica_groups=mesh['seq'=32,'head'=4] {'seq','head'}, use_global_device_ids=true, to_apply=%region_13.14 | all-reduce | flops 64 | bytes 512 | tf_op jit(solution)/shard_map/psum | solution.py:95
  205.0 72.0 %all-reduce.4.cloned.1.call-done = f32[64,256]{1,0:T(8,128)} async-done(((f32[64,256]{1,0:T(8,128)}), f32[64,256]{1,0:T(8,128)}) %all-reduce.4.cloned.1.call-update) | async-done | bytes 65552 | tf_op jit(solution)/shard_map/psum | solution.py:95
  276.9 1.8 fusion.69
  278.8 1.1 fusion.97
  279.9 2.4 fusion.103
  282.5 1.3 convolution_convert_fusion.5
  283.8 1.1 fusion.100
  284.9 0.6 copy-done.7
  285.5 0.8 fusion.81
  286.4 0.9 fusion.91
  287.3 63.8 %psum.45 = f32[64]{0:T(128)S(1)} all-reduce(f32[64]{0:T(128)S(1)} %fusion.91), channel_id=1, replica_groups=mesh['seq'=32,'head'=4] {'seq','head'}, use_global_device_ids=true, to_apply=%region_19.20 | all-reduce | flops 64 | bytes 512 | tf_op jit(solution)/shard_map/psum | solution.py:95
  351.1 69.9 %all-reduce.6.cloned.1.call-done = f32[64,256]{1,0:T(8,128)} async-done(((f32[64,256]{1,0:T(8,128)}), f32[64,256]{1,0:T(8,128)}) %all-reduce.6.cloned.1.call-update) | async-done | bytes 65552 | tf_op jit(solution)/shard_map/psum | solution.py:95
  421.1 1.8 fusion.66
  422.9 1.1 fusion.95
  424.0 2.4 fusion.104
  426.7 1.3 convolution_convert_fusion.4
  427.9 1.1 fusion.101
  429.0 0.6 copy-done.8
  429.7 0.8 fusion.76
  430.5 0.9 fusion.92
  431.4 63.7 %psum.47 = f32[64]{0:T(128)S(1)} all-reduce(f32[64]{0:T(128)S(1)} %fusion.92), channel_id=1, replica_groups=mesh['seq'=32,'head'=4] {'seq','head'}, use_global_device_ids=true, to_apply=%region_25.26 | all-reduce | flops 64 | bytes 512 | tf_op jit(solution)/shard_map/psum | solution.py:95
  495.1 70.1 %all-reduce.8.cloned.1.call-done = f32[64,256]{1,0:T(8,128)} async-done(((f32[64,256]{1,0:T(8,128)}), f32[64,256]{1,0:T(8,128)}) %all-reduce.8.cloned.1.call-update) | async-done | bytes 65552 | tf_op jit(solution)/shard_map/psum | solution.py:95
  565.2 1.8 fusion.63
  567.0 1.6 fusion.30
  (54 shorter events, 1.2 us)
Async XLA Ops:
  7.2 49.4 %copy-start = (bf16[1536,1152]{1,0:T(8,128)(2,1)S(1)}, bf16[1536,1152]{1,0:T(8,128)(2,1)}, u32[]{:S(2)}) copy-start(bf16[1536,1152]{1,0:T(8,128)(2,1)} %param.16) | copy-start | bytes 10616836
  7.2 45.5 %all-gather.2.cloned.1.call-start = ((), (), s32[]{:S(2)}) async-start(), calls=%async_computation.1 | async-start | bytes 3932160 | tf_op jit(solution)/shard_map/all_gather | solution.py:48
  7.9 126.3 %reduce-scatter.2.cloned.1.call-start = ((), (), s32[]{:S(2)}) async-start(), calls=%async_computation.2 | async-start | bytes 3932160 | tf_op jit(solution)/shard_map/reduce_scatter | solution.py:72
  9.0 47.5 %copy-start.12 = (f32[1536]{0:T(1024)S(1)}, f32[1536]{0:T(1024)}, u32[]{:S(2)}) copy-start(f32[1536]{0:T(1024)} %param.15) | copy-start | bytes 18436
  52.7 2.8 copy-start.1
  95.5 40.9 %copy-start.13 = (f32[1536]{0:T(1024)S(1)}, f32[1536]{0:T(1024)}, u32[]{:S(2)}) copy-start(f32[1536]{0:T(1024)} %param.19) | copy-start | bytes 18436
  95.5 181.4 %all-reduce.4.cloned.1.call-start = ((), (), s32[]{:S(2)}) async-start(), calls=%async_computation.3 | async-start | bytes 131072 | tf_op jit(solution)/shard_map/psum | solution.py:95
  134.3 2.2 copy-start.10
  134.3 2.7 copy-start.11
  136.1 1.4 copy-start.2
  136.1 1.3 copy-start.9
  136.9 0.7 copy-start.5
  137.4 0.6 copy-start.14
  137.7 0.6 copy-start.6
  139.1 282.0 %all-reduce.6.cloned.1.call-start = ((), (), s32[]{:S(2)}) async-start(), calls=%async_computation.4 | async-start | bytes 131072 | tf_op jit(solution)/shard_map/psum | solution.py:95
  276.9 8.6 %copy-start.15 = (bf16[256,256]{1,0:T(8,128)(2,1)S(1)}, bf16[256,256]{1,0:T(8,128)(2,1)}, u32[]{:S(2)}) copy-start(bf16[256,256]{1,0:T(8,128)(2,1)} %copy-done.14) | copy-start | bytes 393220
  279.9 2.6 copy-start.3
  284.9 0.6 copy-start.7
  286.3 278.9 %all-reduce.8.cloned.1.call-start = ((), (), s32[]{:S(2)}) async-start(), calls=%async_computation.5 | async-start | bytes 131072 | tf_op jit(solution)/shard_map/psum | solution.py:95
  421.1 8.6 %copy-start.16 = (bf16[256,256]{1,0:T(8,128)(2,1)S(1)}, bf16[256,256]{1,0:T(8,128)(2,1)}, u32[]{:S(2)}) copy-start(bf16[256,256]{1,0:T(8,128)(2,1)} %copy-done.14) | copy-start | bytes 393220
  424.0 2.6 copy-start.4
  429.0 0.6 copy-start.8
Sparse Core Ops, SparseCore 0:
  9.7 42.9 all-gather.1
  95.7 38.5 reduce-scatter.1
  139.6 137.3 all-reduce.3
  286.4 134.5 all-reduce.5
  430.6 134.5 all-reduce.7
where the time goes:
time: 576 us; the launch traced here: 575 us
  waiting for transfers between devices  289 us (50%)
  blocking collectives  192 us (33%)
  matrix products  51.3 us (9%)
  other arithmetic  14.7 us (3%)
  between operations  14.1 us (2%)
  local copies, waits for them, and re-layouts  13.7 us (2%)
    psum x3, waiting for transfers between devices, local(): numer, denom = lax.psum((numer, denom), ('seq', 'head'))  212 us
    psum x3, blocking collectives, local(): numer, denom = lax.psum((numer, denom), ('seq', 'head'))  192 us
    all_gather x1, waiting for transfers between devices, local(): whole = lax.all_gather(tokens, 'head', axis=1, tiled=True)  43.7 us
    reduce_scatter x1, waiting for transfers between devices, local(): lax.psum_scatter(jnp.dot(attended, w_out, preferred_element_type=jnp.floa...  32.3 us
  transfers between devices with their start and end apart: 5, of which 5 were waited for; matrix products, arithmetic and copies ran while one was open for 2% of the time, Pallas kernels for 0%

commit v1 on v0

--- a/solution.py
+++ b/solution.py
@@ -1,11 +1,20 @@
+import functools
+
 import jax
 import jax.numpy as jnp
 from jax import lax
+from jax.experimental import pallas as pl
+from jax.experimental.pallas import tpu as pltpu
 from jax.sharding import PartitionSpec as P
 
 HD = 64
 ITERS = 3
 BLK = 64
+NX, NY, NC, NZ = 4, 4, 2, 4
+NG = NZ * NC
+NP = NX * NY
+HIGH = lax.Precision.HIGHEST
+MESH = pl.DeviceIdType.MESH
 
 
 def layer_norm(values, gain):
@@ -15,20 +24,175 @@
     return centred * lax.rsqrt(var + 1e-06) * gain
 
 
+def plain_norm(values):
+    mean = jnp.mean(values, axis=-1, keepdims=True)
+    centred = values - mean
+    var = jnp.mean(centred * centred, axis=-1, keepdims=True)
+    return centred * lax.rsqrt(var + 1e-06)
+
+
 def normalize_exp(scores):
     powers = jnp.exp(scores)
     return powers / jnp.sum(powers, axis=-1, keepdims=True)
 
 
-def recurrent_cell(update, state, w_input, w_hidden):
-    high = lax.Precision.HIGHEST
-    width = state.shape[1]
-    from_in = jnp.dot(update, w_input, precision=high)
-    from_state = jnp.dot(state, w_hidden, precision=high)
-    reset = jax.nn.sigmoid(from_in[:, :width] + from_state[:, :width])
-    gate = jax.nn.sigmoid(from_in[:, width : 2 * width] + from_state[:, width : 2 * width])
-    candidate = jnp.tanh(from_in[:, 2 * width :] + reset * from_state[:, 2 * width :])
-    return (1.0 - gate) * candidate + gate * state
+def where_am_i():
+    seq, z = lax.axis_index("seq"), lax.axis_index("head")
+    core = lax.rem(seq, NC)
+    place = lax.div(seq, NC)
+    return seq, z, core, place
+
+
+def slot_kernel(
+    keys_ref, values_ref, init_ref, wq_ref, wi_ref, wh_ref, out_ref,
+    part, rs_buf, ar_buf, ag_buf, rs_send, rs_recv, ar_send, ar_recv, ag_send, ag_recv,
+):
+    seq, z, core, place = where_am_i()
+    group = z * NC + core
+    width = init_ref.shape[1]
+    own = init_ref.shape[0] // NG
+
+    def group_peer(step):
+        peer = lax.rem(group + step, NG)
+        return peer, (place * NC + lax.rem(peer, NC), lax.div(peer, NC))
+
+    def plane_peer(step):
+        peer = lax.rem(place + step, NP)
+        return peer, (peer * NC + core, z)
+
+    barrier = pltpu.get_barrier_semaphore()
+    for step in range(1, NG):
+        pl.semaphore_signal(barrier, inc=1, device_id=group_peer(step)[1], device_id_type=MESH)
+    for step in range(1, NP):
+        pl.semaphore_signal(barrier, inc=1, device_id=plane_peer(step)[1], device_id_type=MESH)
+
+    start = pl.multiple_of(group * own, own)
+    state = init_ref[pl.ds(start, own), :]
+    query = jnp.dot(
+        plain_norm(init_ref[...]), wq_ref[...], precision=HIGH, preferred_element_type=jnp.float32
+    ).astype(jnp.bfloat16)
+    pl.semaphore_wait(barrier, NG - 1 + NP - 1)
+
+    sent = []
+    for it in range(ITERS):
+        logits = lax.dot_general(
+            query, keys_ref[...], (((1,), (1,)), ((), ())), preferred_element_type=jnp.float32
+        ) * width ** (-0.5)
+        powers = jnp.exp(logits)
+        weights = powers / jnp.sum(powers, axis=0, keepdims=True)
+        part[it, :, :width] = jnp.dot(
+            weights.astype(jnp.bfloat16), values_ref[...], preferred_element_type=jnp.float32
+        )
+        denom = jnp.sum(weights, axis=1, keepdims=True)
+        part[it, :, width:] = jnp.broadcast_to(denom, (denom.shape[0], 128))
+
+        def rs_copy(step, peer, device):
+            return pltpu.make_async_remote_copy(
+                src_ref=part.at[it, pl.ds(pl.multiple_of(peer * own, own), own), :],
+                dst_ref=rs_buf.at[it, step],
+                send_sem=rs_send.at[it, step],
+                recv_sem=rs_recv.at[it, step],
+                device_id=device,
+                device_id_type=MESH,
+            )
+
+        copies = [rs_copy(step, *group_peer(step)) for step in range(1, NG)]
+        for copy in copies:
+            copy.start()
+        sent += copies
+        from_state = jnp.dot(state, wh_ref[...], precision=HIGH, preferred_element_type=jnp.float32)
+        total = part[it, pl.ds(start, own), :]
+        for copy in copies:
+            copy.wait_recv()
+        for step in range(1, NG):
+            total = total + rs_buf[it, step]
+
+        ar_buf[it, place] = total
+
+        def ar_copy(step, device):
+            return pltpu.make_async_remote_copy(
+                src_ref=ar_buf.at[it, place],
+                dst_ref=ar_buf.at[it, place],
+                send_sem=ar_send.at[it, step],
+                recv_sem=ar_recv.at[it, step],
+                device_id=device,
+                device_id_type=MESH,
+            )
+
+        copies = [ar_copy(step, plane_peer(step)[1]) for step in range(1, NP)]
+        for copy in copies:
+            copy.start()
+        sent += copies
+        for copy in copies:
+            copy.wait_recv()
+        total = ar_buf[it, 0]
+        for peer in range(1, NP):
+            total = total + ar_buf[it, peer]
+
+        update = total[:, :width] / total[:, width : width + 1]
+        from_in = jnp.dot(update, wi_ref[...], precision=HIGH, preferred_element_type=jnp.float32)
+        reset = jax.nn.sigmoid(from_in[:, :width] + from_state[:, :width])
+        gate = jax.nn.sigmoid(
+            from_in[:, width : 2 * width] + from_state[:, width : 2 * width]
+        )
+        candidate = jnp.tanh(from_in[:, 2 * width :] + reset * from_state[:, 2 * width :])
+        state = (1.0 - gate) * candidate + gate * state
+        if it < ITERS - 1:
+            message = jnp.dot(
+                plain_norm(state), wq_ref[...], precision=HIGH, preferred_element_type=jnp.float32
+            )
+        else:
+            message = state
+        ag_buf[it, pl.ds(start, own), :] = message
+
+        def ag_copy(step, device):
+            return pltpu.make_async_remote_copy(
+                src_ref=ag_buf.at[it, pl.ds(start, own), :],
+                dst_ref=ag_buf.at[it, pl.ds(start, own), :],
+                send_sem=ag_send.at[it, step],
+                recv_sem=ag_recv.at[it, step],
+                device_id=device,
+                device_id_type=MESH,
+            )
+
+        copies = [ag_copy(step, group_peer(step)[1]) for step in range(1, NG)]
+        for copy in copies:
+            copy.start()
+        sent += copies
+        for copy in copies:
+            copy.wait_recv()
+        if it < ITERS - 1:
+            query = ag_buf[it].astype(jnp.bfloat16)
+        else:
+            out_ref[...] = ag_buf[it]
+    for copy in sent:
+        copy.wait_send()
+
+
+def slot_attention(keys, values, slot_init, w_query, w_input, w_hidden):
+    slots, width = slot_init.shape
+    own = slots // NG
+    vmem = pl.BlockSpec(memory_space=pltpu.VMEM)
+    return pl.pallas_call(
+        slot_kernel,
+        out_shape=jax.ShapeDtypeStruct((slots, width), jnp.float32),
+        in_specs=[vmem] * 6,
+        out_specs=vmem,
+        scratch_shapes=[
+            pltpu.VMEM((ITERS, slots, width + 128), jnp.float32),
+            pltpu.VMEM((ITERS, NG, own, width + 128), jnp.float32),
+            pltpu.VMEM((ITERS, NP, own, width + 128), jnp.float32),
+            pltpu.VMEM((ITERS, slots, width), jnp.float32),
+            pltpu.SemaphoreType.DMA((ITERS, NG)),
+            pltpu.SemaphoreType.DMA((ITERS, NG)),
+            pltpu.SemaphoreType.DMA((ITERS, NP)),
+            pltpu.SemaphoreType.DMA((ITERS, NP)),
+            pltpu.SemaphoreType.DMA((ITERS, NG)),
+            pltpu.SemaphoreType.DMA((ITERS, NG)),
+        ],
+        compiler_params=pltpu.CompilerParams(collective_id=0, has_side_effects=True),
+        name="slot_attention",
+    )(keys, values, slot_init, w_query, w_input, w_hidden)
 
 
 def local(
@@ -79,21 +243,7 @@
     slot_in = layer_norm(mixed.astype(jnp.float32), slot_gain).astype(jnp.bfloat16)
     keys = jnp.dot(slot_in, w_key, preferred_element_type=jnp.float32).astype(jnp.bfloat16)
     values = jnp.dot(slot_in, w_value, preferred_element_type=jnp.float32).astype(jnp.bfloat16)
-    slots = slot_init
-    width = slot_init.shape[1]
-    ones = jnp.ones((width,), jnp.float32)
-    for step in range(ITERS):
-        query = jnp.dot(layer_norm(slots, ones), w_query, precision=lax.Precision.HIGHEST).astype(
-            jnp.bfloat16
-        )
-        logits = jnp.dot(keys, query.T, preferred_element_type=jnp.float32) * width ** (-0.5)
-        weights = normalize_exp(logits)
-        numer = jnp.einsum(
-            "ts,td->sd", weights.astype(jnp.bfloat16), values, preferred_element_type=jnp.float32
-        )
-        denom = jnp.sum(weights, axis=0)
-        numer, denom = lax.psum((numer, denom), ("seq", "head"))
-        slots = recurrent_cell(numer / denom[:, None], slots, w_input, w_hidden)
+    slots = slot_attention(keys, values, slot_init, w_query, w_input, w_hidden)
     return (mixed, slots)
 
 

time: 576 us -> 200 us (0.35)
  waiting for transfers between devices: 289 us -> 83.1 us
  blocking collectives: 192 us -> 0 us
  Pallas kernels: 0 us -> 52.3 us
  matrix products: 51.3 us -> 30.7 us
  other arithmetic: 14.7 us -> 5.65 us
    psum x3 -> x0, waiting for transfers between devices: 212 us -> none  [local(): numer, denom = lax.psum((numer, denom), ('seq', 'head'))]
    psum x3 -> x0, blocking collectives: 192 us -> none  [local(): numer, denom = lax.psum((numer, denom), ('seq', 'head'))]
    pallas_call x0 -> x1, Pallas kernels: none -> 52.3 us  [slot_attention(): pl.pallas_call(slot_kernel, out_shape=jax.ShapeDtypeStruct((slots, width)...]
    dot_general x15 -> x0, matrix products: 21.9 us -> none  [the longest x3 7.3 us: recurrent_cell(): from_state = jnp.dot(state, w_hidden, precision=high)]
    reduce_scatter x1, waiting for transfers between devices: 32.3 us -> 38.7 us  [local(): lax.psum_scatter(jnp.dot(attended, w_out, preferred_element_type=jnp.floa...]
  transfers between devices with their start and end apart: 5 -> 2, of which waited for: 5 -> 2; matrix products, arithmetic and copies ran while one was open for 2% -> 1% of each run, Pallas kernels for 0% -> 0%
where the time goes in v1:
time: 200 us; the launch traced here: 199 us
  waiting for transfers between devices  83.1 us (42%)
  Pallas kernels  52.3 us (26%)
  matrix products  30.7 us (15%)
  between operations  14.1 us (7%)
  local copies, waits for them, and re-layouts  13.3 us (7%)
  other arithmetic  5.65 us (3%)
    pallas_call x1, Pallas kernels, slot_attention(): pl.pallas_call(slot_kernel, out_shape=jax.ShapeDtypeStruct((slots, width)...  52.3 us
    all_gather x1, waiting for transfers between devices, local(): whole = lax.all_gather(tokens, 'head', axis=1, tiled=True)  43.7 us
    reduce_scatter x1, waiting for transfers between devices, local(): lax.psum_scatter(jnp.dot(attended, w_out, preferred_element_type=jnp.floa...  38.7 us
    dot_general x6, matrix products, one_head(): jnp.dot(probs, head_qkv[:, 2, :], preferred_element_type=jnp.float32)  11 us
    dot_general x6, matrix products, one_head(): jnp.dot(head_qkv[:, 0, :], head_qkv[:, 1, :].T, preferred_element_type=jn...  6.62 us
    squeeze x6, local copies, waits for them, and re-layouts, local(): outputs = lax.map(one_head, split)  6.13 us
    dot_general x1, matrix products, local(): jnp.dot(normed, w_qkv, preferred_element_type=jnp.float32)  5.82 us
    dot_general x1, matrix products, local(): jnp.dot(attended, w_out, preferred_element_type=jnp.float32)  5.05 us
  transfers between devices with their start and end apart: 2, of which 2 were waited for; matrix products, arithmetic and copies ran while one was open for 1% of the time, Pallas kernels for 0%

profile of v1, /device:TPU:1, one launch (start us, length us, event | category | flops | bytes accessed | tf_op | source)
XLA Modules:
  0.0 199.3 jit_solution(4498117165814697621)
XLA Ops:
  7.2 0.0 copy-start
  7.2 0.0 all-gather.2.cloned.1.call-start
  7.2 0.7 all-gather.2.cloned.1.call-update
  7.9 0.0 reduce-scatter.2.cloned.1.call-start
  8.0 1.0 broadcast_in_dim.22
  9.0 0.1 eq.15
  9.0 0.0 copy-start.5
  9.0 43.7 %all-gather.2.cloned.1.call-done = bf16[1024,1536]{1,0:T(8,128)(2,1)} async-done(((bf16[1024,384]{1,0:T(8,128)(2,1)}), bf16[1024,1536]{1,0:T(8,128)(2,1)}) %all-gather.2.cloned.1.call-update) | async-done | bytes 3145744 | tf_op jit(solution)/shard_map/all_gather | solution.py:212
  52.7 0.0 copy-start.1
  52.7 2.5 %convert_reduce_fusion = f32[1024]{0:T(1024)S(1)} fusion(bf16[1024,1536]{1,0:T(8,128)(2,1)} %all-gather.2.cloned.1.call-done), kind=kLoop, calls=%fused_computation.16 | loop fusion | flops 3144704 | bytes 3149824 | tf_op jit(solution)/shard_map/reduce_sum | solution.py:21
  55.3 0.3 copy-done.1
  55.6 1.0 fusion.12
  56.5 0.0 copy-done
  56.5 0.0 copy-done.5
  56.5 5.8 %convolution_convert_fusion.1 = bf16[1024,1152]{1,0:T(8,128)(2,1)} fusion(bf16[1536,1152]{1,0:T(8,128)(2,1)S(1)} %copy-done, bf16[1024,1536]{1,0:T(8,128)(2,1)S(1)} %copy-done.1, f32[1536]{0:T(1024)S(1)} %copy-done.5, f32[1024]{0:T(1024)S(1)} %add_rsqrt_fusion, f32[1024]{0:T(1024)S(1)} %broadcast_multiply_fusion), kind=kOutput, calls=%fused_computation.23 | convolution fusion | flops 3632922624 | bytes 9058304 | tf_op jit(solution)/shard_map/dot_general | solution.py:215
  62.4 4.3 %copy.15 = bf16[1024,1152]{0,1:T(8,128)(2,1)} copy(bf16[1024,1152]{1,0:T(8,128)(2,1)} %convolution_convert_fusion.1) | data formatting | bytes 4718592 | tf_op jit(solution)/shard_map/convert_element_type | solution.py:215
  66.7 23.8 %while.11 = (s32[]{:T(128)}, bf16[6,1024,64]{1,2,0:T(8,128)(2,1)}, bf16[6,1024,3,64]{1,3,2,0:T(8,128)(2,1)}, s32[1024]{0:T(1024)S(1)}, s32[]{:T(128)}) while((s32[]{:T(128)}, bf16[6,1024,64]{1,2,0:T(8,128)(2,1)}, bf16[6,1024,3,64]{1,3,2,0:T(8,128)(2,1)}, s32[1024]{0:T(1024)S(1)}, s32[]{:T(128)}) %tuple.38), condition=%wide.region_4.5_spmd.clone, body=%wide.region_2.4_spmd.clone.sunk | while | flops 277937152 | bytes 9724481 | solution.py:231
  66.7 1.0 dynamic-slice_bitcast_fusion.2
  67.7 1.1 fusion.33
  68.8 1.8 fusion.34
  70.6 1.0 dynamic-slice_bitcast_fusion.2
  71.7 1.1 fusion.33
  72.8 1.8 fusion.34
  74.6 1.0 dynamic-slice_bitcast_fusion.2
  75.6 1.1 fusion.33
  76.7 1.8 fusion.34
  78.6 1.0 dynamic-slice_bitcast_fusion.2
  79.6 1.1 fusion.33
  80.7 1.8 fusion.34
  82.5 1.0 dynamic-slice_bitcast_fusion.2
  83.6 1.1 fusion.33
  84.7 1.8 fusion.34
  86.5 1.0 dynamic-slice_bitcast_fusion.2
  87.5 1.1 fusion.33
  88.6 1.8 fusion.34
  90.5 5.0 %convolution_convert_fusion = bf16[1024,1536]{1,0:T(8,128)(2,1)} fusion(bf16[1024,384]{0,1:T(8,128)(2,1)} %bitcast.4, bf16[384,1536]{1,0:T(8,128)(2,1)} %param.17), kind=kOutput, calls=%fused_computation.22 | convolution fusion | flops 1209532416 | bytes 5111808 | tf_op jit(solution)/shard_map/dot_general | solution.py:237
  95.5 0.0 copy-start.6
  95.5 0.0 reduce-scatter.2.cloned.1.call-update
  95.6 38.7 %reduce-scatter.2.cloned.1.call-done = bf16[256,1536]{1,0:T(8,128)(2,1)} async-done(((bf16[1024,1536]{1,0:T(8,128)(2,1)}), bf16[256,1536]{1,0:T(8,128)(2,1)}) %reduce-scatter.2.cloned.1.call-update) | async-done | bytes 786448 | tf_op jit(solution)/shard_map/reduce_scatter | solution.py:236
  134.3 0.0 copy-start.3
  134.3 0.0 copy-start.4
  134.3 1.8 convert_reduce_fusion.1
  136.1 0.0 copy-start.2
  136.1 0.3 fusion.21
  136.4 0.0 copy-done.6
  136.5 0.0 copy-done.3
  136.5 1.1 convolution_convert_fusion.2.values_ref
  137.6 0.0 copy-done.2
  137.6 0.0 copy-done.4
  137.6 1.1 convolution_convert_fusion.3.keys_ref
  138.7 52.3 %slot_attention.1 = f32[64,256]{1,0:T(8,128)} custom-call(bf16[256,256]{1,0:T(8,128)(2,1)} %convolution_convert_fusion.3.keys_ref, bf16[256,256]{1,0:T(8,128)(2,1)} %convolution_convert_fusion.2.values_ref, f32[64,256]{1,0:T(8,128)} %init_ref.1, f32[256,256]{1,0:T(8,128)} %wq_ref.1, f32[256,768]{1,0:T(8,128)} %wi_ref.1, f32[256,768]{1,0:T(8,128)} %wh_ref.1), custom_call_target="tpu_custom_call" | custom-call | tf_op jit(solution)/shard_map/slot_attention/pallas_call | solution.py:176
  191.0 1.5 copy.24
  (5 shorter events, 0.0 us)
Async XLA Ops:
  7.2 49.4 %copy-start = (bf16[1536,1152]{1,0:T(8,128)(2,1)S(1)}, bf16[1536,1152]{1,0:T(8,128)(2,1)}, u32[]{:S(2)}) copy-start(bf16[1536,1152]{1,0:T(8,128)(2,1)} %param.16) | copy-start | bytes 10616836
  7.2 45.5 %all-gather.2.cloned.1.call-start = ((), (), s32[]{:S(2)}) async-start(), calls=%async_computation.1 | async-start | bytes 3932160 | tf_op jit(solution)/shard_map/all_gather | solution.py:212
  7.9 126.3 %reduce-scatter.2.cloned.1.call-start = ((), (), s32[]{:S(2)}) async-start(), calls=%async_computation.2 | async-start | bytes 3932160 | tf_op jit(solution)/shard_map/reduce_scatter | solution.py:236
  9.0 47.5 %copy-start.5 = (f32[1536]{0:T(1024)S(1)}, f32[1536]{0:T(1024)}, u32[]{:S(2)}) copy-start(f32[1536]{0:T(1024)} %param.15) | copy-start | bytes 18436
  52.7 2.8 %copy-start.1 = (bf16[1024,1536]{1,0:T(8,128)(2,1)S(1)}, bf16[1024,1536]{1,0:T(8,128)(2,1)}, u32[]{:S(2)}) copy-start(bf16[1024,1536]{1,0:T(8,128)(2,1)} %all-gather.2.cloned.1.call-done) | copy-start | bytes 9437188
  95.5 40.9 %copy-start.6 = (f32[1536]{0:T(1024)S(1)}, f32[1536]{0:T(1024)}, u32[]{:S(2)}) copy-start(f32[1536]{0:T(1024)} %param.19) | copy-start | bytes 18436
  134.3 2.2 %copy-start.3 = (bf16[1536,256]{1,0:T(8,128)(2,1)S(1)}, bf16[1536,256]{1,0:T(8,128)(2,1)}, u32[]{:S(2)}) copy-start(bf16[1536,256]{1,0:T(8,128)(2,1)} %param.21) | copy-start | bytes 2359300
  134.3 3.3 %copy-start.4 = (bf16[1536,256]{1,0:T(8,128)(2,1)S(1)}, bf16[1536,256]{1,0:T(8,128)(2,1)}, u32[]{:S(2)}) copy-start(bf16[1536,256]{1,0:T(8,128)(2,1)} %param.20) | copy-start | bytes 2359300
  136.1 1.5 copy-start.2
Sparse Core Ops, SparseCore 0:
  9.7 42.9 all-gather.1
  95.7 38.5 reduce-scatter.1

commit v2 on v1

v2 whole, which is shorter than its diff:
```python
import functools

import jax
import jax.numpy as jnp
from jax import lax
from jax.experimental import pallas as pl
from jax.experimental.pallas import tpu as pltpu
from jax.sharding import PartitionSpec as P

HD = 64
ITERS = 3
BLK = 64
NX, NY, NC, NZ = 4, 4, 2, 4
NG = NZ * NC
NP = NX * NY
CHUNKS = 4
REACH = 3 * BLK
LAG = 2
HIGH = lax.Precision.HIGHEST
MESH = pl.DeviceIdType.MESH


def plain_norm(values):
    mean = jnp.mean(values, axis=-1, keepdims=True)
    centred = values - mean
    var = jnp.mean(centred * centred, axis=-1, keepdims=True)
    return centred * lax.rsqrt(var + 1e-06)


def block_kernel(
    tokens_ref, wqkv_ref, wout_ref, ids_ref, ngain_ref, sgain_ref, wk_ref, wv_ref,
    init_ref, wq_ref, wi_ref, wh_ref, mixed_ref, slots_ref,
    whole, wqkv, wfull, qkv, att_out, att_in, keys_buf, values_buf,
    part, rs_buf, ar_buf, ag_buf,
    load_sem, own_sem, tok_send, tok_recv, att_send, att_recv, w_send, w_recv,
    rs_send, rs_recv, ar_send, ar_recv, ag_send, ag_recv,
):
    z = lax.axis_index("head")
    seq = lax.axis_index("seq")
    core = lax.rem(seq, NC)
    place = lax.div(seq, NC)
    px, py = lax.div(place, NY), lax.rem(place, NY)
    group = z * NC + core
    rows, cols = tokens_ref.shape
    width = init_ref.shape[1]
    own = init_ref.shape[0] // NG
    chunk = rows // CHUNKS
    half = chunk // 2
    right, left = lax.rem(z + 1, NZ), lax.rem(z + NZ - 1, NZ)

    def device(x, y, c, zz):
        return ((x * NY + y) * NC + c, zz)

    def group_peer(step):
        peer = lax.rem(group + step, NG)
        return peer, (place * NC + lax.rem(peer, NC), lax.div(peer, NC))

    def plane_peer(step):
        peer = lax.rem(place + step, NP)
        return peer, (peer * NC + core, z)

    def remote(src, dst, send, recv, target):
        return pltpu.make_async_remote_copy(
            src_ref=src, dst_ref=dst, send_sem=send, recv_sem=recv,
            device_id=target, device_id_type=MESH,
        )

    barrier = pltpu.get_barrier_semaphore()
    for step in range(1, NG):
        pl.semaphore_signal(barrier, inc=1, device_id=group_peer(step)[1], device_id_type=MESH)
    for step in range(1, NP):
        pl.semaphore_signal(barrier, inc=1, device_id=plane_peer(step)[1], device_id_type=MESH)

    def col(zz):
        return pl.ds(pl.multiple_of(zz * cols, cols), cols)

    load_tokens = pltpu.make_async_copy(tokens_ref, whole.at[:, col(z)], load_sem.at[0])
    load_qkv = pltpu.make_async_copy(wqkv_ref, wqkv, load_sem.at[1])
    load_out = pltpu.make_async_copy(wout_ref, wfull.at[z], load_sem.at[2])
    load_tokens.start()
    load_qkv.start()
    load_out.start()

    start = pl.multiple_of(group * own, own)
    query = jnp.dot(
        plain_norm(init_ref[...]), wq_ref[...], precision=HIGH, preferred_element_type=jnp.float32
    ).astype(jnp.bfloat16)
    pl.semaphore_wait(barrier, NG - 1 + NP - 1)

    def chunk_rows(c):
        return pl.ds(pl.multiple_of(c * chunk, chunk), chunk)

    def own_copy(c, way):
        return remote(
            tokens_ref.at[chunk_rows(c), :],
            whole.at[chunk_rows(c), col(z)],
            tok_send.at[way, c],
            tok_recv.at[way, c],
            (seq, right if way == 0 else left),
        )

    def forward_copy(c, way):
        part_rows = pl.ds(pl.multiple_of(c * chunk + way * half, half), half)
        source = left if way == 0 else right
        return remote(
            whole.at[part_rows, col(source)],
            whole.at[part_rows, col(source)],
            tok_send.at[2 + way, c],
            tok_recv.at[2 + way, c],
            (seq, right if way == 0 else left),
        )

    share = wfull.shape[3]
    wide = wfull.shape[4] // NY
    my_cols = pl.ds(pl.multiple_of(py * wide, wide), wide)

    def first_copy(dz):
        return remote(
            wout_ref.at[px, core, :, my_cols],
            wfull.at[z, px, core, :, my_cols],
            w_send.at[0, dz],
            w_recv.at[0, dz],
            (seq, lax.rem(z + dz, NZ)),
        )

    def x_peer(d):
        return (lax.rem(px + d, NX) * NY + py) * NC + core, z

    def y_peer(d):
        return (px * NY + lax.rem(py + d, NY)) * NC + core, z

    def plane_copy(stage, dz, d):
        zz = lax.rem(z + dz, NZ)
        index = (dz - 1) * 3 + d - 1
        if stage == 1:
            ref = wfull.at[zz, px, core, :, my_cols]
            target = (
                jnp.where(core == 0, x_peer(d)[0], y_peer(d)[0]),
                z,
            )
            return remote(ref, ref, w_send.at[1, index], w_recv.at[1, index], target)
        if stage == 2:
            ref = wfull.at[zz, :, 0, :, my_cols]
            return remote(ref, ref, w_send.at[2, index], w_recv.at[2, index], y_peer(d))
        ref = wfull.at[zz, px, 1, :, :]
        return remote(ref, ref, w_send.at[2, index], w_recv.at[2, index], x_peer(d))

    def last_copy(dz):
        zz = lax.rem(z + dz, NZ)
        ref = wfull.at[zz, :, core, :, :]
        return remote(
            ref, ref, w_send.at[3, dz], w_recv.at[3, dz], (place * NC + 1 - core, z)
        )

    pairs = [(dz, d) for dz in range(1, NZ) for d in range(1, 4)]

    for way in range(2):
        own_copy(0, way).start()
    for dz in range(1, NZ):
        first_copy(dz).start()
    for way in range(2):
        own_copy(1, way).start()

    heads = cols // HD
    span = chunk + 2 * REACH
    qkv[2 * chunk : span, :] = jnp.zeros((span - 2 * chunk, qkv.shape[1]), jnp.bfloat16)
    load_tokens.wait()
    load_qkv.wait()
    lane_block = lax.broadcasted_iota(jnp.int32, (1, span), 1) // BLK

    def attended_copy(c, pair):
        lanes = pl.ds(pair * 2 * HD, 2 * HD)
        there = pl.ds(pl.multiple_of(z * cols + pair * 2 * HD, 2 * HD), 2 * HD)
        return remote(
            att_out.at[chunk_rows(c), lanes],
            att_in.at[:, there],
            att_send.at[c, pair],
            att_recv.at[z, pair],
            (seq, c),
        )

    def project(c):
        x = whole[chunk_rows(c), :].astype(jnp.float32)
        normed = (plain_norm(x) * ngain_ref[...]).astype(jnp.bfloat16)
        qkv[chunk_rows(c), :] = jnp.dot(
            normed, wqkv[...], preferred_element_type=jnp.float32
        ).astype(jnp.bfloat16)

    def attend(c):
        first = pl.multiple_of(jnp.clip(c * chunk - REACH, 0, rows - span), BLK)
        first_block = first // BLK
        key_ids = jnp.zeros((1, span), jnp.int32)
        for b in range(span // BLK):
            key_ids = jnp.where(lane_block == b, ids_ref[0, first_block + b], key_ids)
        same = [
            key_ids == ids_ref[0, c * (chunk // BLK) + b] for b in range(chunk // BLK)
        ]
        for pair in range(heads // 2):
            outputs = []
            for h in range(2):
                base = (2 * pair + h) * 3 * HD
                q = qkv[chunk_rows(c), base : base + HD]
                k = qkv[pl.ds(first, span), base + HD : base + 2 * HD]
                v = qkv[pl.ds(first, span), base + 2 * HD : base + 3 * HD]
                scores = lax.dot_general(
                    q, k, (((1,), (1,)), ((), ())), preferred_element_type=jnp.float32
                )
                probs = []
                for b in range(chunk // BLK):
                    powers = jnp.where(
                        same[b], jnp.exp(scores[b * BLK : (b + 1) * BLK] * HD ** (-0.5)), 0.0
                    )
                    inverse = 1.0 / jnp.sum(powers, axis=-1, keepdims=True)
                    probs.append((powers * inverse).astype(jnp.bfloat16))
                outputs.append(
                    jnp.dot(
                        jnp.concatenate(probs, axis=0), v, preferred_element_type=jnp.float32
                    ).astype(jnp.bfloat16)
                )
            both = jnp.concatenate(outputs, axis=1)

            @pl.when(c == z)
            def _():
                lanes = pl.ds(pl.multiple_of(z * cols + pair * 2 * HD, 2 * HD), 2 * HD)
                att_in[:, lanes] = both

            @pl.when(c != z)
            def _():
                att_out[chunk_rows(c), pair * 2 * HD : (pair + 1) * 2 * HD] = both
                attended_copy(c, pair).start()

    @pl.loop(0, CHUNKS + LAG)
    def _(c):
        @pl.when(c < CHUNKS)
        def _():
            for way in range(2):
                own_copy(c, way).wait_recv()
            for way in range(2):
                forward_copy(c, way).start()

            @pl.when(c + 2 < CHUNKS)
            def _():
                for way in range(2):
                    own_copy(c + 2, way).start()

        @pl.when(c == 0)
        def _():
            for dz in range(1, NZ):
                first_copy(dz).wait_recv()
            for dz, d in pairs:
                plane_copy(1, dz, d).start()

        @pl.when(c == 1)
        def _():
            for dz, d in pairs:
                plane_copy(1, dz, d).wait_recv()

            @pl.when(core == 0)
            def _():
                for dz, d in pairs:
                    plane_copy(2, dz, d).start()

            @pl.when(core == 1)
            def _():
                for dz, d in pairs:
                    plane_copy(3, dz, d).start()

        @pl.when(c >= LAG)
        def _():
            attend(c - LAG)

        @pl.when(c < CHUNKS)
        def _():
            for way in range(2):
                forward_copy(c, way).wait_recv()
            project(c)

        @pl.when(c == CHUNKS - 1)
        def _():
            @pl.when(core == 0)
            def _():
                for dz, d in pairs:
                    plane_copy(2, dz, d).wait_recv()

            @pl.when(core == 1)
            def _():
                for dz, d in pairs:
                    plane_copy(3, dz, d).wait_recv()

            for dz in range(1, NZ):
                last_copy(dz).start()

    load_out.wait()
    for dz in range(1, NZ):
        last_copy(dz).wait_recv()
    for dz in range(1, NZ):
        source = lax.rem(z + dz, NZ)
        for pair in range(heads // 2):
            lanes = pl.ds(pl.multiple_of(source * cols + pair * 2 * HD, 2 * HD), 2 * HD)
            remote(
                att_in.at[:, lanes], att_in.at[:, lanes], att_send.at[source, pair],
                att_recv.at[source, pair], (seq, source),
            ).wait_recv()

    projected = jnp.dot(
        att_in[...],
        wfull[...].reshape(wfull.shape[4], wfull.shape[4]),
        preferred_element_type=jnp.float32,
    )
    mixed = (whole[chunk_rows(z), :].astype(jnp.float32) + projected).astype(jnp.bfloat16)
    mixed_ref[...] = mixed
    slot_in = (plain_norm(mixed.astype(jnp.float32)) * sgain_ref[...]).astype(jnp.bfloat16)
    keys_buf[...] = jnp.dot(slot_in, wk_ref[...], preferred_element_type=jnp.float32).astype(
        jnp.bfloat16
    )
    values_buf[...] = jnp.dot(slot_in, wv_ref[...], preferred_element_type=jnp.float32).astype(
        jnp.bfloat16
    )

    state = init_ref[pl.ds(start, own), :]
    sent = []
    for it in range(ITERS):
        logits = lax.dot_general(
            query, keys_buf[...], (((1,), (1,)), ((), ())), preferred_element_type=jnp.float32
        ) * width ** (-0.5)
        powers = jnp.exp(logits)
        weights = powers / jnp.sum(powers, axis=0, keepdims=True)
        part[it, :, :width] = jnp.dot(
            weights.astype(jnp.bfloat16), values_buf[...], preferred_element_type=jnp.float32
        )
        denom = jnp.sum(weights, axis=1, keepdims=True)
        part[it, :, width:] = jnp.broadcast_to(denom, (denom.shape[0], 128))

        copies = []
        for step in range(1, NG):
            peer, target = group_peer(step)
            copies.append(
                remote(
                    part.at[it, pl.ds(pl.multiple_of(peer * own, own), own), :],
                    rs_buf.at[it, step],
                    rs_send.at[it, step],
                    rs_recv.at[it, step],
                    target,
                )
            )
        for copy in copies:
            copy.start()
        sent += copies
        from_state = jnp.dot(state, wh_ref[...], precision=HIGH, preferred_element_type=jnp.float32)
        total = part[it, pl.ds(start, own), :]
        for copy in copies:
            copy.wait_recv()
        for step in range(1, NG):
            total = total + rs_buf[it, step]

        ar_buf[it, place] = total
        copies = [
            remote(
                ar_buf.at[it, place],
                ar_buf.at[it, place],
                ar_send.at[it, step],
                ar_recv.at[it, step],
                plane_peer(step)[1],
            )
            for step in range(1, NP)
        ]
        for copy in copies:
            copy.start()
        sent += copies
        for copy in copies:
            copy.wait_recv()
        total = ar_buf[it, 0]
        for peer in range(1, NP):
            total = total + ar_buf[it, peer]

        update = total[:, :width] / total[:, width : width + 1]
        from_in = jnp.dot(update, wi_ref[...], precision=HIGH, preferred_element_type=jnp.float32)
        reset = jax.nn.sigmoid(from_in[:, :width] + from_state[:, :width])
        gate = jax.nn.sigmoid(
            from_in[:, width : 2 * width] + from_state[:, width : 2 * width]
        )
        candidate = jnp.tanh(from_in[:, 2 * width :] + reset * from_state[:, 2 * width :])
        state = (1.0 - gate) * candidate + gate * state
        if it < ITERS - 1:
            message = jnp.dot(
                plain_norm(state), wq_ref[...], precision=HIGH, preferred_element_type=jnp.float32
            )
        else:
            message = state
        ag_buf[it, pl.ds(start, own), :] = message
        copies = [
            remote(
                ag_buf.at[it, pl.ds(start, own), :],
                ag_buf.at[it, pl.ds(start, own), :],
                ag_send.at[it, step],
                ag_recv.at[it, step],
                group_peer(step)[1],
            )
            for step in range(1, NG)
        ]
        for copy in copies:
            copy.start()
        sent += copies
        for copy in copies:
            copy.wait_recv()
        if it < ITERS - 1:
            query = ag_buf[it].astype(jnp.bfloat16)
        else:
            slots_ref[...] = ag_buf[it]

    for copy in sent:
        copy.wait_send()

    @pl.loop(0, CHUNKS)
    def _(c):
        for way in range(2):
            own_copy(c, way).wait_send()
            forward_copy(c, way).wait_send()

        @pl.when(c != z)
        def _():
            for pair in range(heads // 2):
                attended_copy(c, pair).wait_send()

    for dz in range(1, NZ):
        first_copy(dz).wait_send()
        last_copy(dz).wait_send()
    for dz, d in pairs:
        plane_copy(1, dz, d).wait_send()

    @pl.when(core == 0)
    def _():
        for dz, d in pairs:
            plane_copy(2, dz, d).wait_send()

    @pl.when(core == 1)
    def _():
        for dz, d in pairs:
            plane_copy(3, dz, d).wait_send()


def local(
    tokens,
    norm_gain,
    w_qkv,
    w_out,
    frame_ids,
    slot_gain,
    w_key,
    w_value,
    w_query,
    slot_init,
    w_input,
    w_hidden,
):
    rows, cols = tokens.shape
    full = cols * NZ
    slots, width = slot_init.shape
    own = slots // NG
    chunk = rows // CHUNKS
    vmem = pl.BlockSpec(memory_space=pltpu.VMEM)
    hbm = pl.BlockSpec(memory_space=pl.ANY)
    share = cols // (NX * NC)
    dma = pltpu.SemaphoreType.DMA
    return pl.pallas_call(
        block_kernel,
        out_shape=(
            jax.ShapeDtypeStruct((chunk, full), jnp.bfloat16),
            jax.ShapeDtypeStruct((slots, width), jnp.float32),
        ),
        in_specs=[hbm, hbm, hbm, pl.BlockSpec(memory_space=pltpu.SMEM)] + [vmem] * 8,
        out_specs=(vmem, vmem),
        scratch_shapes=[
            pltpu.VMEM((rows, full), jnp.bfloat16),
            pltpu.VMEM(w_qkv.shape, jnp.bfloat16),
            pltpu.VMEM((NZ, NX, NC, share, full), jnp.bfloat16),
            pltpu.VMEM((rows, w_qkv.shape[1]), jnp.bfloat16),
            pltpu.VMEM((rows, cols), jnp.bfloat16),
            pltpu.VMEM((chunk, full), jnp.bfloat16),
            pltpu.VMEM((chunk, width), jnp.bfloat16),
            pltpu.VMEM((chunk, width), jnp.bfloat16),
            pltpu.VMEM((ITERS, slots, width + 128), jnp.float32),
            pltpu.VMEM((ITERS, NG, own, width + 128), jnp.float32),
            pltpu.VMEM((ITERS, NP, own, width + 128), jnp.float32),
            pltpu.VMEM((ITERS, slots, width), jnp.float32),
            dma((3,)),
            dma((1,)),
            dma((4, CHUNKS)),
            dma((4, CHUNKS)),
            dma((CHUNKS, 3)),
            dma((NZ, 3)),
            dma((4, 9)),
            dma((4, 9)),
            dma((ITERS, NG)),
            dma((ITERS, NG)),
            dma((ITERS, NP)),
            dma((ITERS, NP)),
            dma((ITERS, NG)),
            dma((ITERS, NG)),
        ],
        compiler_params=pltpu.CompilerParams(
            collective_id=0, has_side_effects=True, vmem_limit_bytes=60 * 1024 * 1024
        ),
        name="vision_block",
    )(
        tokens,
        w_qkv,
        w_out.reshape(NX, NC, share, full),
        frame_ids,
        norm_gain.reshape(1, full),
        slot_gain.reshape(1, full),
        w_key,
        w_value,
        slot_init,
        w_query,
        w_input,
        w_hidden,
    )


def solution(mesh):
    placed = (
        P("seq", "head"),
        P(),
        P(None, "head"),
        P("head", None),
        P("seq", None),
        P(),
        P(),
        P(),
        P(),
        P(),
        P(),
        P(),
    )
    return jax.shard_map(
        local,
        mesh=mesh,
        in_specs=placed,
        out_specs=(P(("seq", "head"), None), P()),
        check_vma=False,
    )
```

time: 200 us -> 119 us (0.59)
  waiting for transfers between devices: 83.1 us -> 0 us
  Pallas kernels: 52.3 us -> 112 us
  matrix products: 30.7 us -> 0 us
  between operations: 14.1 us -> 0.64 us
  local copies, waits for them, and re-layouts: 13.3 us -> 6.12 us
  other arithmetic: 5.65 us -> 0 us
    pallas_call x1, Pallas kernels: 52.3 us -> 112 us  [local(): pl.pallas_call(block_kernel, out_shape=(jax.ShapeDtypeStruct((chunk, full...]
    all_gather x1 -> x0, waiting for transfers between devices: 43.7 us -> none  [local(): whole = lax.all_gather(tokens, 'head', axis=1, tiled=True)]
    reduce_scatter x1 -> x0, waiting for transfers between devices: 38.7 us -> none  [local(): lax.psum_scatter(jnp.dot(attended, w_out, preferred_element_type=jnp.floa...]
    dot_general x16 -> x0, matrix products: 30.7 us -> none  [the longest x6 11 us: one_head(): jnp.dot(probs, head_qkv[:, 2, :], preferred_element_type=jnp.float32)]
    squeeze x6 -> x0, local copies, waits for them, and re-layouts: 6.13 us -> none  [local(): outputs = lax.map(one_head, split)]
    reduce_sum x4 -> x0, other arithmetic: 5.62 us -> none  [the longest x2 4.31 us: layer_norm(): mean = jnp.mean(values, axis=-1, keepdims=True)]
    convert_element_type x1 -> x0, local copies, waits for them, and re-layouts: 4.28 us -> none  [local(): jnp.dot(normed, w_qkv, preferred_element_type=jnp.float32)]
    reshape x0 -> x2, local copies, waits for them, and re-layouts: none -> 2.59 us  [the longest x1 1.3 us: local(): norm_gain.reshape(1, full)]
  transfers between devices with their start and end apart: 2 -> 0, of which waited for: 2 -> 0; matrix products, arithmetic and copies ran while one was open for 1% -> 0% of each run, Pallas kernels for 0% -> 0%
where the time goes in v2:
time: 119 us
  Pallas kernels  112 us (94%)
  local copies, waits for them, and re-layouts  6.12 us (5%)
    pallas_call x1, Pallas kernels, local(): pl.pallas_call(block_kernel, out_shape=(jax.ShapeDtypeStruct((chunk, full...  112 us
    unnamed x2, local copies, waits for them, and re-layouts  3.54 us

profile of v2, /device:TPU:1, one launch (start us, length us, event | category | flops | bytes accessed | tf_op | source)
XLA Modules:
  0.0 119.1 jit_solution(3118737669557783464)
XLA Ops:
  0.6 1.3 %reshape.14.ngain_ref = f32[1,1536]{1,0:T(1,128)} reshape(f32[1536]{0:T(1024)} %param.13) | data formatting | bytes 12288 | tf_op jit(solution)/shard_map/reshape | solution.py:510
  1.9 1.3 %reshape.15.sgain_ref = f32[1,1536]{1,0:T(1,128)} reshape(f32[1536]{0:T(1024)} %param.17) | data formatting | bytes 12288 | tf_op jit(solution)/shard_map/reshape | solution.py:511
  3.2 112.3 %vision_block.1 = (bf16[256,1536]{1,0:T(8,128)(2,1)}, f32[64,256]{1,0:T(8,128)}) custom-call(bf16[1024,384]{1,0:T(8,128)(2,1)} %tokens_ref.1, bf16[1536,1152]{1,0:T(8,128)(2,1)} %wqkv_ref.1, bf16[4,2,48,1536]{3,2,1,0:T(8,128)(2,1)} %bitcast.1, s32[1,16]{1,0:T(1,128)} %ids_ref.1, f32[1,1536]{1,0:T(1,128)} %reshape.14.ngain_ref, f32[1,1536]{1,0:T(1,128)} %reshape.15.sgain_ref, ...), custom_call_target="tpu_custom_call" | custom-call | tf_op jit(solution)/shard_map/vision_block/pallas_call | solution.py:465
  115.5 2.1 %copy.16 = bf16[256,1536]{1,0:T(8,128)(2,1)} copy(bf16[256,1536]{1,0:T(8,128)(2,1)} %get-tuple-element.4) | data formatting | bytes 1572864
  117.6 1.5 %copy.17 = f32[64,256]{1,0:T(8,128)} copy(f32[64,256]{1,0:T(8,128)} %get-tuple-element.5) | data formatting | bytes 131072

commit v3 on v2

--- a/solution.py
+++ b/solution.py
@@ -28,10 +28,10 @@
 
 
 def block_kernel(
-    tokens_ref, wqkv_ref, wout_ref, ids_ref, ngain_ref, sgain_ref, wk_ref, wv_ref,
-    init_ref, wq_ref, wi_ref, wh_ref, mixed_ref, slots_ref,
+    tokens_ref, wqkv_ref, wout_ref, wk_hbm, wv_hbm, wi_hbm, wh_hbm, ids_ref, ngain_ref,
+    sgain_ref, init_ref, wq_ref, mixed_ref, slots_ref,
     whole, wqkv, wfull, qkv, att_out, att_in, keys_buf, values_buf,
-    part, rs_buf, ar_buf, ag_buf,
+    part, rs_buf, ar_buf, ag_buf, wk_ref, wv_ref, wi_ref, wh_ref,
     load_sem, own_sem, tok_send, tok_recv, att_send, att_recv, w_send, w_recv,
     rs_send, rs_recv, ar_send, ar_recv, ag_send, ag_recv,
 ):
@@ -80,6 +80,14 @@
     load_tokens.start()
     load_qkv.start()
     load_out.start()
+    late = [
+        pltpu.make_async_copy(src, dst, load_sem.at[3 + i])
+        for i, (src, dst) in enumerate(
+            [(wk_hbm, wk_ref), (wv_hbm, wv_ref), (wi_hbm, wi_ref), (wh_hbm, wh_ref)]
+        )
+    ]
+    for copy in late:
+        copy.start()
 
     start = pl.multiple_of(group * own, own)
     query = jnp.dot(
@@ -181,7 +189,7 @@
 
     def project(c):
         x = whole[chunk_rows(c), :].astype(jnp.float32)
-        normed = (plain_norm(x) * ngain_ref[...]).astype(jnp.bfloat16)
+        normed = (plain_norm(x) * ngain_ref[...].reshape(1, -1)).astype(jnp.bfloat16)
         qkv[chunk_rows(c), :] = jnp.dot(
             normed, wqkv[...], preferred_element_type=jnp.float32
         ).astype(jnp.bfloat16)
@@ -291,6 +299,8 @@
                 last_copy(dz).start()
 
     load_out.wait()
+    for copy in late:
+        copy.wait()
     for dz in range(1, NZ):
         last_copy(dz).wait_recv()
     for dz in range(1, NZ):
@@ -309,7 +319,7 @@
     )
     mixed = (whole[chunk_rows(z), :].astype(jnp.float32) + projected).astype(jnp.bfloat16)
     mixed_ref[...] = mixed
-    slot_in = (plain_norm(mixed.astype(jnp.float32)) * sgain_ref[...]).astype(jnp.bfloat16)
+    slot_in = (plain_norm(mixed.astype(jnp.float32)) * sgain_ref[...].reshape(1, -1)).astype(jnp.bfloat16)
     keys_buf[...] = jnp.dot(slot_in, wk_ref[...], preferred_element_type=jnp.float32).astype(
         jnp.bfloat16
     )
@@ -439,6 +449,11 @@
             plane_copy(3, dz, d).wait_send()
 
 
+def finish_kernel(mixed_ref, slots_ref, mixed_out, slots_out):
+    mixed_out[...] = mixed_ref[...]
+    slots_out[...] = slots_ref[...]
+
+
 def local(
     tokens,
     norm_gain,
@@ -462,13 +477,13 @@
     hbm = pl.BlockSpec(memory_space=pl.ANY)
     share = cols // (NX * NC)
     dma = pltpu.SemaphoreType.DMA
-    return pl.pallas_call(
+    results = pl.pallas_call(
         block_kernel,
         out_shape=(
             jax.ShapeDtypeStruct((chunk, full), jnp.bfloat16),
             jax.ShapeDtypeStruct((slots, width), jnp.float32),
         ),
-        in_specs=[hbm, hbm, hbm, pl.BlockSpec(memory_space=pltpu.SMEM)] + [vmem] * 8,
+        in_specs=[hbm] * 7 + [pl.BlockSpec(memory_space=pltpu.SMEM)] + [vmem] * 4,
         out_specs=(vmem, vmem),
         scratch_shapes=[
             pltpu.VMEM((rows, full), jnp.bfloat16),
@@ -483,7 +498,11 @@
             pltpu.VMEM((ITERS, NG, own, width + 128), jnp.float32),
             pltpu.VMEM((ITERS, NP, own, width + 128), jnp.float32),
             pltpu.VMEM((ITERS, slots, width), jnp.float32),
-            dma((3,)),
+            pltpu.VMEM(w_key.shape, jnp.bfloat16),
+            pltpu.VMEM(w_value.shape, jnp.bfloat16),
+            pltpu.VMEM(w_input.shape, jnp.float32),
+            pltpu.VMEM(w_hidden.shape, jnp.float32),
+            dma((7,)),
             dma((1,)),
             dma((4, CHUNKS)),
             dma((4, CHUNKS)),
@@ -506,16 +525,23 @@
         tokens,
         w_qkv,
         w_out.reshape(NX, NC, share, full),
-        frame_ids,
-        norm_gain.reshape(1, full),
-        slot_gain.reshape(1, full),
         w_key,
         w_value,
+        w_input,
+        w_hidden,
+        frame_ids,
+        norm_gain,
+        slot_gain,
         slot_init,
         w_query,
-        w_input,
-        w_hidden,
     )
+    return pl.pallas_call(
+        finish_kernel,
+        out_shape=tuple(jax.ShapeDtypeStruct(r.shape, r.dtype) for r in results),
+        in_specs=[vmem] * 2,
+        out_specs=(vmem,) * 2,
+        name="finish",
+    )(*results)
 
 
 def solution(mesh):

time: 119 us -> 114 us (0.958)
  local copies, waits for them, and re-layouts: 6.12 us -> 0 us
    unnamed x2 -> x0, local copies, waits for them, and re-layouts: 3.54 us -> none
    reshape x2 -> x0, local copies, waits for them, and re-layouts: 2.59 us -> none  [the longest x1 1.3 us: local(): norm_gain.reshape(1, full)]
    pallas_call x0 -> x1, Pallas kernels: none -> 2.08 us  [local(): pl.pallas_call(finish_kernel, out_shape=tuple((jax.ShapeDtypeStruct(r.sha...]
where the time goes in v3:
time: 114 us
  Pallas kernels  113 us (99%)
    pallas_call x1, Pallas kernels, local(): pl.pallas_call(block_kernel, out_shape=(jax.ShapeDtypeStruct((chunk, full...  111 us

profile of v3, /device:TPU:1, one launch (start us, length us, event | category | flops | bytes accessed | tf_op | source)
XLA Modules:
  0.0 114.1 jit_solution(4924381802332346659)
XLA Ops:
  0.6 111.4 %vision_block.1 = (bf16[256,1536]{1,0:T(8,128)(2,1)}, f32[64,256]{1,0:T(8,128)}) custom-call(bf16[1024,384]{1,0:T(8,128)(2,1)} %tokens_ref.1, bf16[1536,1152]{1,0:T(8,128)(2,1)} %wqkv_ref.1, bf16[4,2,48,1536]{3,2,1,0:T(8,128)(2,1)} %bitcast.1, bf16[1536,256]{1,0:T(8,128)(2,1)} %wk_hbm.1, bf16[1536,256]{1,0:T(8,128)(2,1)} %wv_hbm.1, f32[256,768]{1,0:T(8,128)} %wi_hbm.1, ...), custom_call_target="tpu_custom_call" | custom-call | tf_op jit(solution)/shard_map/vision_block/pallas_call | solution.py:480
  112.0 2.1 %finish.1 = (bf16[256,1536]{1,0:T(8,128)(2,1)}, f32[64,256]{1,0:T(8,128)}) custom-call(bf16[256,1536]{1,0:T(8,128)(2,1)} %get-tuple-element.4.mixed_ref, f32[64,256]{1,0:T(8,128)} %get-tuple-element.5.slots_ref), custom_call_target="tpu_custom_call" | custom-call | tf_op jit(solution)/shard_map/finish/pallas_call | solution.py:538

commit v4 on v3

--- a/solution.py
+++ b/solution.py
@@ -31,9 +31,9 @@
     tokens_ref, wqkv_ref, wout_ref, wk_hbm, wv_hbm, wi_hbm, wh_hbm, ids_ref, ngain_ref,
     sgain_ref, init_ref, wq_ref, mixed_ref, slots_ref,
     whole, wqkv, wfull, qkv, att_out, att_in, keys_buf, values_buf,
-    part, rs_buf, ar_buf, ag_buf, wk_ref, wv_ref, wi_ref, wh_ref,
+    relay, part, rs_buf, ar_buf, ag_buf, wk_ref, wv_ref, wi_ref, wh_ref,
     load_sem, own_sem, tok_send, tok_recv, att_send, att_recv, w_send, w_recv,
-    rs_send, rs_recv, ar_send, ar_recv, ag_send, ag_recv,
+    half_send, half_recv, last_send, last_recv, rs_send, rs_recv, ar_send, ar_recv, ag_send, ag_recv,
 ):
     z = lax.axis_index("head")
     seq = lax.axis_index("seq")
@@ -169,11 +169,23 @@
     for way in range(2):
         own_copy(1, way).start()
 
+    def pass_on(c):
+        for way in range(2):
+            own_copy(c, way).wait_recv()
+        for way in range(2):
+            forward_copy(c, way).start()
+
+        @pl.when(c + 2 < CHUNKS)
+        def _():
+            for way in range(2):
+                own_copy(c + 2, way).start()
+
     heads = cols // HD
     span = chunk + 2 * REACH
     qkv[2 * chunk : span, :] = jnp.zeros((span - 2 * chunk, qkv.shape[1]), jnp.bfloat16)
     load_tokens.wait()
     load_qkv.wait()
+    pass_on(0)
     lane_block = lax.broadcasted_iota(jnp.int32, (1, span), 1) // BLK
 
     def attended_copy(c, pair):
@@ -186,6 +198,38 @@
             att_recv.at[z, pair],
             (seq, c),
         )
+
+    def half_copy(c, way, pair):
+        lanes = pl.ds(pair * 2 * HD, 2 * HD)
+        return remote(
+            att_out.at[pl.ds(pl.multiple_of(c * chunk + way * half, half), half), lanes],
+            relay.at[way, :, lanes],
+            half_send.at[way, pair],
+            half_recv.at[way, pair],
+            (seq, right if way == 0 else left),
+        )
+
+    def relay_copy(way, pair):
+        source = left if way == 0 else right
+        there = pl.ds(pl.multiple_of(source * cols + pair * 2 * HD, 2 * HD), 2 * HD)
+        return remote(
+            relay.at[way, :, pl.ds(pair * 2 * HD, 2 * HD)],
+            att_in.at[pl.ds(way * half, half), there],
+            last_send.at[way, pair],
+            last_recv.at[way, pair],
+            (seq, right if way == 0 else left),
+        )
+
+    def pass_attended(c):
+        for way in range(2):
+
+            @pl.when(c == (right if way == 0 else left))
+            def _():
+                for pair in range(heads // 2):
+                    half_copy(c, way, pair).wait_recv()
+                    relay_copy(way, pair).start()
+
+    opposite = lax.rem(z + 2, NZ)
 
     def project(c):
         x = whole[chunk_rows(c), :].astype(jnp.float32)
@@ -235,21 +279,23 @@
             @pl.when(c != z)
             def _():
                 att_out[chunk_rows(c), pair * 2 * HD : (pair + 1) * 2 * HD] = both
-                attended_copy(c, pair).start()
+
+                @pl.when(c != opposite)
+                def _():
+                    attended_copy(c, pair).start()
+
+                @pl.when(c == opposite)
+                def _():
+                    for way in range(2):
+                        half_copy(c, way, pair).start()
 
     @pl.loop(0, CHUNKS + LAG)
     def _(c):
         @pl.when(c < CHUNKS)
         def _():
-            for way in range(2):
-                own_copy(c, way).wait_recv()
-            for way in range(2):
-                forward_copy(c, way).start()
-
-            @pl.when(c + 2 < CHUNKS)
-            def _():
-                for way in range(2):
-                    own_copy(c + 2, way).start()
+            @pl.when(c + 1 < CHUNKS)
+            def _():
+                pass_on(c + 1)
 
         @pl.when(c == 0)
         def _():
@@ -277,6 +323,10 @@
         def _():
             attend(c - LAG)
 
+        @pl.when(c > LAG)
+        def _():
+            pass_attended(c - LAG - 1)
+
         @pl.when(c < CHUNKS)
         def _():
             for way in range(2):
@@ -298,12 +348,13 @@
             for dz in range(1, NZ):
                 last_copy(dz).start()
 
+    pass_attended(CHUNKS - 1)
     load_out.wait()
     for copy in late:
         copy.wait()
     for dz in range(1, NZ):
         last_copy(dz).wait_recv()
-    for dz in range(1, NZ):
+    for dz in (1, NZ - 1):
         source = lax.rem(z + dz, NZ)
         for pair in range(heads // 2):
             lanes = pl.ds(pl.multiple_of(source * cols + pair * 2 * HD, 2 * HD), 2 * HD)
@@ -311,6 +362,10 @@
                 att_in.at[:, lanes], att_in.at[:, lanes], att_send.at[source, pair],
                 att_recv.at[source, pair], (seq, source),
             ).wait_recv()
+
+    for way in range(2):
+        for pair in range(heads // 2):
+            relay_copy(way, pair).wait_recv()
 
     projected = jnp.dot(
         att_in[...],
@@ -427,10 +482,15 @@
             own_copy(c, way).wait_send()
             forward_copy(c, way).wait_send()
 
-        @pl.when(c != z)
+        @pl.when((c != z) & (c != opposite))
         def _():
             for pair in range(heads // 2):
                 attended_copy(c, pair).wait_send()
+
+    for way in range(2):
+        for pair in range(heads // 2):
+            half_copy(opposite, way, pair).wait_send()
+            relay_copy(way, pair).wait_send()
 
     for dz in range(1, NZ):
         first_copy(dz).wait_send()
@@ -494,6 +554,7 @@
             pltpu.VMEM((chunk, full), jnp.bfloat16),
             pltpu.VMEM((chunk, width), jnp.bfloat16),
             pltpu.VMEM((chunk, width), jnp.bfloat16),
+            pltpu.VMEM((2, chunk // 2, cols), jnp.bfloat16),
             pltpu.VMEM((ITERS, slots, width + 128), jnp.float32),
             pltpu.VMEM((ITERS, NG, own, width + 128), jnp.float32),
             pltpu.VMEM((ITERS, NP, own, width + 128), jnp.float32),
@@ -510,6 +571,10 @@
             dma((NZ, 3)),
             dma((4, 9)),
             dma((4, 9)),
+            dma((2, 3)),
+            dma((2, 3)),
+            dma((2, 3)),
+            dma((2, 3)),
             dma((ITERS, NG)),
             dma((ITERS, NG)),
             dma((ITERS, NP)),

time: 114 us -> 110 us (0.965)
  Pallas kernels: 113 us -> 110 us
    pallas_call x1, Pallas kernels: 111 us -> 108 us  [local(): pl.pallas_call(block_kernel, out_shape=(jax.ShapeDtypeStruct((chunk, full...]
where the time goes in v4:
time: 110 us
  Pallas kernels  110 us (100%)
    pallas_call x1, Pallas kernels, local(): pl.pallas_call(block_kernel, out_shape=(jax.ShapeDtypeStruct((chunk, full...  108 us

profile of v4, /device:TPU:1, one launch (start us, length us, event | category | flops | bytes accessed | tf_op | source)
XLA Modules:
  0.0 110.3 jit_solution(14928454011815643207)
XLA Ops:
  0.6 107.6 %vision_block.1 = (bf16[256,1536]{1,0:T(8,128)(2,1)}, f32[64,256]{1,0:T(8,128)}) custom-call(bf16[1024,384]{1,0:T(8,128)(2,1)} %tokens_ref.1, bf16[1536,1152]{1,0:T(8,128)(2,1)} %wqkv_ref.1, bf16[4,2,48,1536]{3,2,1,0:T(8,128)(2,1)} %bitcast.1, bf16[1536,256]{1,0:T(8,128)(2,1)} %wk_hbm.1, bf16[1536,256]{1,0:T(8,128)(2,1)} %wv_hbm.1, f32[256,768]{1,0:T(8,128)} %wi_hbm.1, ...), custom_call_target="tpu_custom_call" | custom-call | tf_op jit(solution)/shard_map/vision_block/pallas_call | solution.py:540
  108.2 2.1 %finish.1 = (bf16[256,1536]{1,0:T(8,128)(2,1)}, f32[64,256]{1,0:T(8,128)}) custom-call(bf16[256,1536]{1,0:T(8,128)(2,1)} %get-tuple-element.4.mixed_ref, f32[64,256]{1,0:T(8,128)} %get-tuple-element.5.slots_ref), custom_call_target="tpu_custom_call" | custom-call | tf_op jit(solution)/shard_map/finish/pallas_call | solution.py:603
